TPU v7x, 128 devices: a whole 4x4x4 slice. The times are simulated.
128 devices in a mesh: dp: 128 (over z, x, y, core).
Axes of the slice: x: 4, y: 4, z: 4, core: 2. Of those that a mesh axis runs over, the one named last changes fastest.
Arguments:
- hidden: bfloat16 [256, 512, 2048], P('dp'), may hold values from -6 to 6
- lengths: int32 [256], P('dp'), may hold values from 1 to 512, 65536 in all
- order: int32 [256], P('dp'), may hold values from 0 to 255, each once
- candidates: int32 [256, 64], replicated, may hold values from 0 to 65535, as said below
- norm_gain: float32 [2048], replicated, may hold values from 0.25 to 1.75
- w_query: bfloat16 [2048, 1024], P('dp'), may hold values from -1 to 1
- w_key: bfloat16 [2048, 1024], P('dp'), may hold values from -1 to 1
- w_value: bfloat16 [2048, 1024], P('dp'), may hold values from -0.125 to 0.125
- w_out: bfloat16 [1024, 2048], P('dp'), may hold values from -0.75 to 0.75
- index_rows: bfloat16 [65536, 2048], P('dp'), may hold values from -0.125 to 0.125
Outputs:
- scores: float32 [256, 64], P('dp')
Inputs may be any that keep to these rules, and one draw needn't show every extreme that they name: The candidates of many texts may all lie in the index rows of one device: in every draw at least half of the texts have all 64 of their candidates in the 512 index rows of one device, the same device for all of them.
All inputs are finite; a program needn't handle non-finite values. No bound on the sum of `lengths` on one device may be relied on, other than what follows from the above.
Results may differ from a plain program's by a relative error of at most 0.005.
Values may be sent and summed in bfloat16 or wider, within the bound.
No kernel may reach another device: no remote copies, remote signals or barrier semaphores. Data moves between devices by JAX's collectives and lax.ppermute only.
A program may use at most 128 MiB of HBM per device.

v0:
```python
import jax
import jax.numpy as jnp
from jax import lax
from jax.sharding import PartitionSpec as P

HEAD = 64


def attend_text(bundle):
    queries, key_side, value_side, length = bundle
    slots = queries.shape[0]
    logits = jnp.einsum("qhd,khd->hqk", queries, key_side, preferred_element_type=jnp.float32)
    valid = jnp.arange(slots, dtype=jnp.int32) < length
    logits = jnp.where(valid[None, None, :], logits, jnp.float32(-1e30))
    probs = jax.nn.softmax(logits, axis=-1).astype(jnp.bfloat16)
    context = jnp.einsum("hqk,khd->qhd", probs, value_side, preferred_element_type=jnp.float32)
    return context.astype(jnp.bfloat16)


def per_device(
    hidden, lengths, order, candidates, norm_gain, w_query, w_key, w_value, w_out, index_rows
):
    texts, lmax, width = hidden.shape
    slots = texts * lmax
    features = w_query.shape[1]
    heads = features // HEAD
    flat = hidden.reshape(slots, width)
    values_f = flat.astype(jnp.float32)
    meansq = jnp.mean(values_f * values_f, axis=-1, keepdims=True)
    normed = (values_f * lax.rsqrt(meansq + 1e-06) * norm_gain).astype(jnp.bfloat16)
    full_query, full_key, full_value = (
        lax.all_gather(w_query, "dp", axis=0, tiled=True),
        lax.all_gather(w_key, "dp", axis=0, tiled=True),
        lax.all_gather(w_value, "dp", axis=0, tiled=True),
    )
    query_sum = jnp.dot(normed, full_query, preferred_element_type=jnp.float32)
    key_sum = jnp.dot(normed, full_key, preferred_element_type=jnp.float32)
    value_sum = jnp.dot(normed, full_value, preferred_element_type=jnp.float32)
    queries = query_sum.astype(jnp.bfloat16).reshape(texts, lmax, heads, HEAD)
    key_side = key_sum.astype(jnp.bfloat16).reshape(texts, lmax, heads, HEAD)
    value_side = value_sum.astype(jnp.bfloat16).reshape(texts, lmax, heads, HEAD)
    context = lax.map(attend_text, (queries, key_side, value_side, lengths)).reshape(
        slots, features
    )
    projected = jnp.dot(
        context, lax.all_gather(w_out, "dp", axis=0, tiled=True), preferred_element_type=jnp.float32
    )
    layer_out = (values_f + projected).reshape(texts, lmax, width)
    valid = jnp.arange(lmax, dtype=jnp.int32)[None, :] < lengths[:, None]
    pooled = (
        jnp.sum(jnp.where(valid[:, :, None], layer_out, jnp.float32(0.0)), axis=1)
        / lengths.astype(jnp.float32)[:, None]
    )
    unit = (pooled * lax.rsqrt(jnp.mean(pooled * pooled, axis=-1, keepdims=True) + 1e-06)).astype(
        jnp.bfloat16
    )
    order_all = lax.all_gather(order, "dp", axis=0, tiled=True)
    cand_proc = candidates[order_all]
    rows_dev = index_rows.shape[0]
    device = lax.axis_index("dp")
    local_scores = lax.dot_general(
        lax.all_gather(unit, "dp", axis=0, tiled=True),
        index_rows,
        (((1,), (1,)), ((), ())),
        preferred_element_type=jnp.float32,
    )
    owner = cand_proc // rows_dev
    within = cand_proc - owner * rows_dev
    picked = jnp.take_along_axis(local_scores, jnp.clip(within, 0, rows_dev - 1), axis=1)
    partial_value = jnp.where(owner == device, picked, jnp.float32(0.0))
    inverse = jnp.argsort(order_all)
    mine = lax.psum_scatter(partial_value, "dp", scatter_dimension=0, tiled=True)
    every_score = lax.all_gather(mine, "dp", axis=0, tiled=True)
    wanted_rows = lax.dynamic_slice_in_dim(inverse, device * texts, texts, 0)
    return every_score[wanted_rows]


def solution(mesh):
    return jax.shard_map(
        per_device,
        mesh=mesh,
        in_specs=(
            P("dp", None, None),
            P("dp"),
            P("dp"),
            P(),
            P(),
            P("dp", None),
            P("dp", None),
            P("dp", None),
            P("dp", None),
            P("dp", None),
        ),
        out_specs=P("dp", None),
        check_vma=False,
    )
```

profile of v0, /device:TPU:1, one launch (start us, length us, event | category | flops | bytes accessed | tf_op | source)
XLA Modules:
  0.0 678.7 jit_solution(16129564787788719315)
XLA Ops:
  6.5 0.0 copy-start
  6.5 0.0 all-gather.8.cloned.1.call-start
  6.5 0.7 all-gather.8.cloned.1.call-update
  7.3 0.0 all-gather.10.cloned.1.call-start
  7.3 0.7 all-gather.10.cloned.1.call-update
  8.0 0.0 all-gather.12.cloned.1.call-start
  8.1 0.7 all-gather.12.cloned.1.call-update
  8.7 0.0 all-gather.14.cloned.1.call-start
  8.8 0.5 all-gather.14.cloned.1.call-update
  9.3 0.0 all-gather.16.cloned.1.call-start
  9.4 1.3 iota_compare_fusion.1
  10.7 1.2 convert_element_type.43
  11.9 3.1 fusion.39
  15.0 0.0 copy-done.2
  15.0 5.2 fusion.41
  20.2 60.4 %all-gather.8.cloned.1.call-done = bf16[2048,1024]{1,0:T(8,128)(2,1)} async-done(((bf16[16,1024]{1,0:T(8,128)(2,1)}), bf16[2048,1024]{1,0:T(8,128)(2,1)}) %all-gather.8.cloned.1.call-update) | async-done | bytes 4194320 | tf_op jit(solution)/shard_map/all_gather | solution.py:34
  80.6 9.3 %convolution_convert_fusion.2 = bf16[1024,1024]{1,0:T(8,128)(2,1)} fusion(bf16[1024,2048]{1,0:T(8,128)(2,1)} %fusion.41, bf16[2048,1024]{1,0:T(8,128)(2,1)} %all-gather.8.cloned.1.call-done), kind=kOutput, calls=%fused_computation.40 | convolution fusion | flops 4296015872 | bytes 10485760 | tf_op jit(solution)/shard_map/dot_general | solution.py:38
  89.8 6.4 reshape.182
  96.3 5.5 copy.30
  101.7 46.1 %all-gather.10.cloned.1.call-done = bf16[2048,1024]{1,0:T(8,128)(2,1)} async-done(((bf16[16,1024]{1,0:T(8,128)(2,1)}), bf16[2048,1024]{1,0:T(8,128)(2,1)}) %all-gather.10.cloned.1.call-update) | async-done | bytes 4194320 | tf_op jit(solution)/shard_map/all_gather | solution.py:32
  147.8 9.3 %convolution_convert_fusion.1 = bf16[1024,1024]{1,0:T(8,128)(2,1)} fusion(bf16[1024,2048]{1,0:T(8,128)(2,1)} %fusion.41, bf16[2048,1024]{1,0:T(8,128)(2,1)} %all-gather.10.cloned.1.call-done), kind=kOutput, calls=%fused_computation.39 | convolution fusion | flops 4296015872 | bytes 10485760 | tf_op jit(solution)/shard_map/dot_general | solution.py:36
  157.1 6.4 reshape.183
  163.6 5.4 copy.31
  169.0 46.2 %all-gather.12.cloned.1.call-done = bf16[2048,1024]{1,0:T(8,128)(2,1)} async-done(((bf16[16,1024]{1,0:T(8,128)(2,1)}), bf16[2048,1024]{1,0:T(8,128)(2,1)}) %all-gather.12.cloned.1.call-update) | async-done | bytes 4194320 | tf_op jit(solution)/shard_map/all_gather | solution.py:33
  215.2 9.3 %convolution_convert_fusion = bf16[1024,1024]{1,0:T(8,128)(2,1)} fusion(bf16[1024,2048]{1,0:T(8,128)(2,1)} %fusion.41, bf16[2048,1024]{1,0:T(8,128)(2,1)} %all-gather.12.cloned.1.call-done), kind=kOutput, calls=%fused_computation.38 | convolution fusion | flops 4296015872 | bytes 10485760 | tf_op jit(solution)/shard_map/dot_general | solution.py:37
  224.5 6.4 reshape.184
  230.9 5.5 copy.32
  236.4 42.3 %while.10 = (s32[]{:T(128)}, bf16[2,512,16,64]{1,3,2,0:T(8,128)(2,1)}, bf16[2,512,16,64]{1,3,2,0:T(8,128)(2,1)}, s32[2]{0:T(128)S(1)}, bf16[2,512,16,64]{1,3,2,0...) while((s32[]{:T(128)}, bf16[2,512,16,64]{1,3,2,0:T(8,128)(2,1)}, ...), condition=%wide.region_4.5_spmd, body=%wide.region_1.4_spmd.sunk | while | flops 1095238656 | bytes 37817436 | solution.py:42
  236.4 0.7 dynamic_slice.62
  237.0 0.7 iota_compare_fusion.3
  237.7 10.8 %fusion.82 = (f32[16,512]{1,0:T(8,128)S(1)}, f32[16,512,512]{1,2,0:T(8,128)}) fusion(pred[512]{0:T(512)(128)(4,1)S(1)} %iota_compare_fusion.3, bf16[2,512,16,64]{1,3,2,0:T(8,128)(2,1)} %get-tuple-element.134, s32[]{:T(128)} %get-tuple-element.122, bf16[2,512,16,64]{1,3,2,0:T(8,128)(2,1)} %get-tuple-element.133), kind=kOutput, calls=%fused_computation.78.clone.1 | convolution fusion | flops 549454336 | bytes 18908672 | tf_op jit(solution)/shard_map/while/body/eval_jaxpr/sub | solution.py:15
  248.5 8.8 %fusion.83 = bf16[2,512,16,64]{1,3,2,0:T(8,128)(2,1)} fusion(bf16[2,512,16,64]{1,3,2,0:T(8,128)(2,1)} %get-tuple-element.123, s32[]{:T(128)} %get-tuple-element.122, f32[16,512,512]{1,2,0:T(8,128)} %get-tuple-element.113, f32[16,512]{1,0:T(8,128)S(1)} %get-tuple-element.114, bf16[2,512,16,64]{1,3,2,0:T(8,128)(2,1)} %get-tuple-element.131), kind=kOutput, calls=%fused_computation.14.clone.1 | convolution fusion | flops 545783808 | bytes 18908160 | tf_op jit(solution)/shard_map/while/body/eval_jaxpr/hqk,khd->qhd/dot_general | solution.py:16
  257.3 0.7 dynamic_slice.62
  257.9 0.7 iota_compare_fusion.3
  258.6 10.8 %fusion.82 = (f32[16,512]{1,0:T(8,128)S(1)}, f32[16,512,512]{1,2,0:T(8,128)}) fusion(pred[512]{0:T(512)(128)(4,1)S(1)} %iota_compare_fusion.3, bf16[2,512,16,64]{1,3,2,0:T(8,128)(2,1)} %get-tuple-element.134, s32[]{:T(128)} %get-tuple-element.122, bf16[2,512,16,64]{1,3,2,0:T(8,128)(2,1)} %get-tuple-element.133), kind=kOutput, calls=%fused_computation.78.clone.1 | convolution fusion | flops 549454336 | bytes 18908672 | tf_op jit(solution)/shard_map/while/body/eval_jaxpr/sub | solution.py:15
  269.4 9.2 %fusion.83 = bf16[2,512,16,64]{1,3,2,0:T(8,128)(2,1)} fusion(bf16[2,512,16,64]{1,3,2,0:T(8,128)(2,1)} %get-tuple-element.123, s32[]{:T(128)} %get-tuple-element.122, f32[16,512,512]{1,2,0:T(8,128)} %get-tuple-element.113, f32[16,512]{1,0:T(8,128)S(1)} %get-tuple-element.114, bf16[2,512,16,64]{1,3,2,0:T(8,128)(2,1)} %get-tuple-element.131), kind=kOutput, calls=%fused_computation.14.clone.1 | convolution fusion | flops 545783808 | bytes 18908160 | tf_op jit(solution)/shard_map/while/body/eval_jaxpr/hqk,khd->qhd/dot_general | solution.py:16
  278.6 3.8 copy.33
  282.4 1.9 copy.42
  284.4 0.0 copy-done.3
  284.4 0.0 copy-start.6
  284.4 9.2 %select_reduce_fusion.1 = f32[2,2048]{1,0:T(2,128)S(1)} fusion(pred[2,512]{1,0:T(4,128)(4,1)S(1)} %copy-done.3, bf16[1024,1024]{0,1:T(8,128)(2,1)} %bitcast.100, bf16[1024,2048]{1,0:T(8,128)(2,1)} %all-gather.14.cloned.1.call-done, bf16[2,512,2048]{2,1,0:T(8,128)(2,1)} %param.12), kind=kOutput, calls=%fused_computation.37 | convolution fusion | flops 4303351808 | bytes 10503168 | tf_op jit(solution)/shard_map/dot_general | solution.py:45
  293.6 0.2 multiply_reduce_fusion
  293.9 0.7 fusion.53
  294.5 0.0 all-gather.16.cloned.1.call-update
  294.6 0.0 all-reduce.4.cloned.1.call-start
  294.6 0.0 copy-done.1
  294.6 0.1 copy.26
  294.7 0.2 dynamic-update-slice
  295.0 63.0 %all-reduce = s32[256]{0:T(256)S(1)} all-reduce(s32[256]{0:T(256)S(1)} %dynamic-update-slice), channel_id=1, replica_groups=mesh['dp'=128] {'dp'}, use_global_device_ids=true, to_apply=%add | all-reduce | flops 256 | bytes 2048
  358.0 0.7 gather_fusion
  358.8 0.1 fusion.49
  358.9 0.1 reshape.168
  359.0 3.2 sort.17
  362.2 0.1 compare_select_fusion.3
  362.3 2.3 reshape.179
  364.5 2.0 fusion.63
  366.5 129.5 %gather_fusion.2 = f32[16384]{0:T(1024)S(1)} fusion(f32[256,512]{1,0:T(8,128)S(1)} %fusion.63, s32[16384]{0:T(1024)S(1)} %reshape.168), kind=kCustom, calls=%fused_computation.2 | custom fusion | bytes 262144 | tf_op jit(solution)/shard_map/jit(take_along_axis)/gather | solution.py:69
  496.0 0.1 reshape.171
  496.1 0.8 select_select_fusion
  496.9 0.0 all-reduce.4.cloned.1.call-update
  496.9 139.4 %all-reduce.4.cloned.1.call-done = f32[256,64]{1,0:T(8,128)} async-done(((f32[256,64]{1,0:T(8,128)}), f32[256,64]{1,0:T(8,128)}) %all-reduce.4.cloned.1.call-update) | async-done | bytes 65552
  636.3 0.7 dynamic-slice_bitcast_fusion
  637.0 33.8 %all-gather.1 = f32[128,2,64]{2,1,0:T(2,128)S(1)} all-gather(f32[1,2,64]{2,1,0:T(2,128)S(1)} %dynamic-slice_bitcast_fusion), channel_id=1, replica_groups=mesh['dp'=128] {'dp'}, dimensions={0}, use_global_device_ids=true | all-gather | bytes 66048 | tf_op jit(solution)/shard_map/all_gather | solution.py:73
  670.8 1.1 gather_fusion.1
  (20 shorter events, 0.1 us)
Async XLA Ops:
  6.5 358.0 %copy-start = (bf16[512,2048]{1,0:T(8,128)(2,1)S(1)}, bf16[512,2048]{1,0:T(8,128)(2,1)}, u32[]{:S(2)}) copy-start(bf16[512,2048]{1,0:T(8,128)(2,1)} %param.21) | copy-start | bytes 6291460
  6.5 8.5 %copy-start.2 = (f32[2048]{0:T(1024)S(1)}, f32[2048]{0:T(1024)}, u32[]{:S(2)}) copy-start(f32[2048]{0:T(1024)} %param.16) | copy-start | bytes 24580
  6.5 74.0 %all-gather.8.cloned.1.call-start = ((), (), s32[]{:S(2)}) async-start(), calls=%async_computation | async-start | bytes 4227072 | tf_op jit(solution)/shard_map/all_gather | solution.py:34
  7.3 140.6 %all-gather.10.cloned.1.call-start = ((), (), s32[]{:S(2)}) async-start(), calls=%async_computation.1 | async-start | bytes 4227072 | tf_op jit(solution)/shard_map/all_gather | solution.py:32
  8.0 207.2 %all-gather.12.cloned.1.call-start = ((), (), s32[]{:S(2)}) async-start(), calls=%async_computation.2 | async-start | bytes 4227072 | tf_op jit(solution)/shard_map/all_gather | solution.py:33
  8.7 275.6 %all-gather.14.cloned.1.call-start = ((), (), s32[]{:S(2)}) async-start(), calls=%async_computation.3 | async-start | bytes 4227072 | tf_op jit(solution)/shard_map/all_gather | solution.py:46
  9.3 352.9 %all-gather.16.cloned.1.call-start = ((), (), s32[]{:S(2)}) async-start(), calls=%async_computation.4 | async-start | bytes 1056768 | tf_op jit(solution)/shard_map/all_gather | solution.py:62
  230.9 5.5 copy-start.5
  278.6 5.7 copy-start.3
  284.4 9.3 %copy-start.4 = (f32[2]{0:T(128)S(1)}, f32[2]{0:T(128)}, u32[]{:S(2)}) copy-start(f32[2]{0:T(128)} %convert_element_type.43) | copy-start | bytes 28
  284.4 10.2 %copy-start.1 = (s32[256,64]{0,1:T(8,128)S(1)}, s32[256,64]{0,1:T(8,128)}, u32[]{:S(2)}) copy-start(s32[256,64]{0,1:T(8,128)} %param.15) | copy-start | bytes 196612
  284.4 10.4 %copy-start.6 = (s32[2]{0:T(128)S(1)}, s32[2]{0:T(128)}, u32[]{:S(2)}) copy-start(s32[2]{0:T(128)} %param.14) | copy-start | bytes 28
  294.6 341.8 %all-reduce.4.cloned.1.call-start = ((), (), s32[]{:S(2)}) async-start(), calls=%async_computation.5 | async-start | bytes 262144
Sparse Core Ops, SparseCore 0:
  10.5 70.0 all-gather.7
  83.7 64.1 all-gather.9
  151.0 64.1 all-gather.11
  218.1 64.1 all-gather.13
  294.7 61.1 all-gather.15
  497.0 139.2 all-reduce.3
where the time goes:
time: 680 us; the launch traced here: 679 us
  waiting for transfers between devices  295 us (43%)
  local copies, waits for them, and re-layouts  177 us (26%)
  blocking collectives  96.8 us (14%)
  matrix products  78.7 us (12%)
  other arithmetic  17.3 us (3%)
  between operations  13.6 us (2%)
    unnamed x7, waiting for transfers between devices  142 us
    gather x3, local copies, waits for them, and re-layouts, per_device(): jnp.take_along_axis(local_scores, jnp.clip(within, 0, rows_dev - 1), axis=1)  130 us
    unnamed x1, blocking collectives  63 us
    all_gather x1, waiting for transfers between devices, per_device(): lax.all_gather(w_value, 'dp', axis=0, tiled=True)  60.4 us
    all_gather x1, waiting for transfers between devices, per_device(): lax.all_gather(w_key, 'dp', axis=0, tiled=True)  46.2 us
    all_gather x1, waiting for transfers between devices, per_device(): lax.all_gather(w_query, 'dp', axis=0, tiled=True)  46.1 us
    all_gather x1, blocking collectives, per_device(): every_score = lax.all_gather(mine, 'dp', axis=0, tiled=True)  33.8 us
    sub x2, matrix products, attend_text(): probs = jax.nn.softmax(logits, axis=-1).astype(jnp.bfloat16)  21.5 us
  transfers between devices with their start and end apart: 6, of which 4 were waited for; matrix products, arithmetic and copies ran while one was open for 19% of the time, Pallas kernels for 0%

commit v1 on v0

--- a/solution.py
+++ b/solution.py
@@ -4,6 +4,15 @@
 from jax.sharding import PartitionSpec as P
 
 HEAD = 64
+
+
+def drive_plate_for(xin):
+    copies = []
+    for _ in range(lax.psum(1, axis_name="dp")):
+        copies.append(xin)
+    return jnp.concatenate(
+        lax.all_to_all(jnp.stack(copies), axis_name="dp", split_axis=0, concat_axis=0), 0
+    )
 
 
 def attend_text(bundle):
@@ -29,7 +38,7 @@
     meansq = jnp.mean(values_f * values_f, axis=-1, keepdims=True)
     normed = (values_f * lax.rsqrt(meansq + 1e-06) * norm_gain).astype(jnp.bfloat16)
     full_query, full_key, full_value = (
-        lax.all_gather(w_query, "dp", axis=0, tiled=True),
+        drive_plate_for(w_query),
         lax.all_gather(w_key, "dp", axis=0, tiled=True),
         lax.all_gather(w_value, "dp", axis=0, tiled=True),
     )

time: 680 us -> 638 us (0.938)
  waiting for transfers between devices: 295 us -> 236 us
  starting transfers between devices: 0.2 us -> 12.1 us
    all_gather x1, waiting for transfers between devices: 60.4 us -> 9.19 us  [per_device(): lax.all_gather(w_value, 'dp', axis=0, tiled=True)]
    all_gather x1 -> x0, waiting for transfers between devices: 46.1 us -> none  [per_device(): lax.all_gather(w_query, 'dp', axis=0, tiled=True)]
    all_to_all x0 -> x1, waiting for transfers between devices: none -> 39.5 us  [drive_plate_for(): lax.all_to_all(jnp.stack(copies), axis_name='dp', split_axis=0, concat_ax...]
    all_to_all x0 -> x1, starting transfers between devices: none -> 11.9 us  [drive_plate_for(): lax.all_to_all(jnp.stack(copies), axis_name='dp', split_axis=0, concat_ax...]
    unnamed x7 -> x6, waiting for transfers between devices: 142 us -> 142 us
  transfers between devices with their start and end apart: 6 -> 6, of which waited for: 4 -> 4; matrix products, arithmetic and copies ran while one was open for 19% -> 21% of each run, Pallas kernels for 0% -> 0%
where the time goes in v1:
time: 638 us; the launch traced here: 637 us
  waiting for transfers between devices  236 us (37%)
  local copies, waits for them, and re-layouts  181 us (28%)
  blocking collectives  96.8 us (15%)
  matrix products  78.6 us (12%)
  other arithmetic  19.1 us (3%)
  between operations  13.3 us (2%)
  starting transfers between devices  12.1 us (2%)
    unnamed x6, waiting for transfers between devices  142 us
    gather x3, local copies, waits for them, and re-layouts, per_device(): jnp.take_along_axis(local_scores, jnp.clip(within, 0, rows_dev - 1), axis=1)  130 us
    unnamed x1, blocking collectives  63 us
    all_gather x1, waiting for transfers between devices, per_device(): lax.all_gather(w_key, 'dp', axis=0, tiled=True)  46 us
    all_to_all x1, waiting for transfers between devices, drive_plate_for(): lax.all_to_all(jnp.stack(copies), axis_name='dp', split_axis=0, concat_ax...  39.5 us
    all_gather x1, blocking collectives, per_device(): every_score = lax.all_gather(mine, 'dp', axis=0, tiled=True)  33.8 us
    sub x2, matrix products, attend_text(): probs = jax.nn.softmax(logits, axis=-1).astype(jnp.bfloat16)  21.6 us
    while x4, local copies, waits for them, and re-layouts, per_device(): lax.map(attend_text, (queries, key_side, value_side, lengths))  20.3 us
  transfers between devices with their start and end apart: 6, of which 4 were waited for; matrix products, arithmetic and copies ran while one was open for 21% of the time, Pallas kernels for 0%

profile of v1, /device:TPU:1, one launch (start us, length us, event | category | flops | bytes accessed | tf_op | source)
XLA Modules:
  0.0 637.1 jit_solution(1819468844518484282)
XLA Ops:
  6.5 0.0 copy-start
  6.5 0.7 all-gather.7.cloned.1.call-update
  7.3 0.0 all-gather.9.cloned.1.call-start
  7.3 0.7 all-gather.9.cloned.1.call-update
  8.0 3.3 stack.2
  11.3 11.9 %all-to-all-start = ((bf16[128,16,1024]{2,1,0:T(8,128)(2,1)}), bf16[128,16,1024]{2,1,0:T(8,128)(2,1)}, u32[]{:S(2)}, u32[]{:S(2)}) async-start(bf16[128,16,1024]{2,1,0:T(8,128)(2,1)} %stack.2), calls=%async_computation | async-start | bytes 8388608 | tf_op jit(solution)/shard_map/all_to_all | solution.py:14
  23.2 0.0 copy-start.6
  23.2 0.0 copy-start.3
  23.2 0.0 all-gather.11.cloned.1.call-start
  23.3 0.7 all-gather.11.cloned.1.call-update
  24.0 0.0 all-gather.13.cloned.1.call-start
  24.0 3.1 fusion.39
  27.2 0.6 convert_element_type.51
  27.8 0.7 iota_compare_fusion.1
  28.4 5.3 fusion.43
  33.7 3.0 fusion.41
  36.7 39.5 %all-to-all-done = bf16[128,16,1024]{2,1,0:T(8,128)(2,1)} async-done(((bf16[128,16,1024]{2,1,0:T(8,128)(2,1)}), bf16[128,16,1024]{2,1,0:T(8,128)(2,1)}, u32[]{:S(2)}, u32[]{:S(2)}) %all-to-all-start) | async-done | bytes 4194336 | tf_op jit(solution)/shard_map/all_to_all | solution.py:14
  76.3 9.3 %convolution_convert_fusion.1 = bf16[1024,1024]{1,0:T(8,128)(2,1)} fusion(bf16[1024,2048]{1,0:T(8,128)(2,1)} %bitcast.102, bf16[2048,1024]{1,0:T(8,128)(2,1)} %bitcast.8), kind=kOutput, calls=%fused_computation.42 | convolution fusion | flops 4296015872 | bytes 10485760 | tf_op jit(solution)/shard_map/dot_general | solution.py:45
  85.6 6.5 %reshape.200 = bf16[2,512,16,64]{3,2,1,0:T(8,128)(2,1)} reshape(bf16[1024,1024]{1,0:T(8,128)(2,1)} %convolution_convert_fusion.1) | data formatting | bytes 4194304 | tf_op jit(solution)/shard_map/reshape | solution.py:48
  92.1 5.6 copy.31
  97.7 9.2 %all-gather.7.cloned.1.call-done = bf16[2048,1024]{1,0:T(8,128)(2,1)} async-done(((bf16[16,1024]{1,0:T(8,128)(2,1)}), bf16[2048,1024]{1,0:T(8,128)(2,1)}) %all-gather.7.cloned.1.call-update) | async-done | bytes 4194320 | tf_op jit(solution)/shard_map/all_gather | solution.py:43
  106.8 9.3 %convolution_convert_fusion.2 = bf16[1024,1024]{1,0:T(8,128)(2,1)} fusion(bf16[1024,2048]{1,0:T(8,128)(2,1)} %fusion.43, bf16[2048,1024]{1,0:T(8,128)(2,1)} %all-gather.7.cloned.1.call-done), kind=kOutput, calls=%fused_computation.43 | convolution fusion | flops 4296015872 | bytes 10485760 | tf_op jit(solution)/shard_map/dot_general | solution.py:47
  116.1 6.4 %reshape.199 = bf16[2,512,16,64]{3,2,1,0:T(8,128)(2,1)} reshape(bf16[1024,1024]{1,0:T(8,128)(2,1)} %convolution_convert_fusion.2) | data formatting | bytes 4194304 | tf_op jit(solution)/shard_map/reshape | solution.py:50
  122.5 5.5 copy.30
  128.0 46.0 %all-gather.9.cloned.1.call-done = bf16[2048,1024]{1,0:T(8,128)(2,1)} async-done(((bf16[16,1024]{1,0:T(8,128)(2,1)}), bf16[2048,1024]{1,0:T(8,128)(2,1)}) %all-gather.9.cloned.1.call-update) | async-done | bytes 4194320 | tf_op jit(solution)/shard_map/all_gather | solution.py:42
  174.0 9.3 %convolution_convert_fusion = bf16[1024,1024]{1,0:T(8,128)(2,1)} fusion(bf16[1024,2048]{1,0:T(8,128)(2,1)} %fusion.43, bf16[2048,1024]{1,0:T(8,128)(2,1)} %all-gather.9.cloned.1.call-done), kind=kOutput, calls=%fused_computation.41 | convolution fusion | flops 4296015872 | bytes 10485760 | tf_op jit(solution)/shard_map/dot_general | solution.py:46
  183.3 6.4 reshape.201
  189.7 5.4 copy.32
  195.1 42.2 %while.10 = (s32[]{:T(128)}, bf16[2,512,16,64]{1,3,2,0:T(8,128)(2,1)}, bf16[2,512,16,64]{1,3,2,0:T(8,128)(2,1)}, s32[2]{0:T(128)S(1)}, bf16[2,512,16,64]{1,3,2,0...) while((s32[]{:T(128)}, bf16[2,512,16,64]{1,3,2,0:T(8,128)(2,1)}, ...), condition=%wide.region_4.5_spmd, body=%wide.region_1.4_spmd.sunk | while | flops 1095238656 | bytes 37817436 | solution.py:51
  195.1 0.6 dynamic_slice.62
  195.8 0.7 iota_compare_fusion.3
  196.5 10.8 %fusion.85 = (f32[16,512]{1,0:T(8,128)S(1)}, f32[16,512,512]{1,2,0:T(8,128)}) fusion(pred[512]{0:T(512)(128)(4,1)S(1)} %iota_compare_fusion.3, bf16[2,512,16,64]{1,3,2,0:T(8,128)(2,1)} %get-tuple-element.136, s32[]{:T(128)} %get-tuple-element.124, bf16[2,512,16,64]{1,3,2,0:T(8,128)(2,1)} %get-tuple-element.135), kind=kOutput, calls=%fused_computation.82.clone.1 | convolution fusion | flops 549454336 | bytes 18908672 | tf_op jit(solution)/shard_map/while/body/eval_jaxpr/sub | solution.py:24
  207.2 8.8 %fusion.86 = bf16[2,512,16,64]{1,3,2,0:T(8,128)(2,1)} fusion(bf16[2,512,16,64]{1,3,2,0:T(8,128)(2,1)} %get-tuple-element.125, s32[]{:T(128)} %get-tuple-element.124, f32[16,512,512]{1,2,0:T(8,128)} %get-tuple-element.115, f32[16,512]{1,0:T(8,128)S(1)} %get-tuple-element.116, bf16[2,512,16,64]{1,3,2,0:T(8,128)(2,1)} %get-tuple-element.133), kind=kOutput, calls=%fused_computation.14.clone.1 | convolution fusion | flops 545783808 | bytes 18908160 | tf_op jit(solution)/shard_map/while/body/eval_jaxpr/hqk,khd->qhd/dot_general | solution.py:25
  216.0 0.6 dynamic_slice.62
  216.7 0.7 iota_compare_fusion.3
  217.3 10.8 %fusion.85 = (f32[16,512]{1,0:T(8,128)S(1)}, f32[16,512,512]{1,2,0:T(8,128)}) fusion(pred[512]{0:T(512)(128)(4,1)S(1)} %iota_compare_fusion.3, bf16[2,512,16,64]{1,3,2,0:T(8,128)(2,1)} %get-tuple-element.136, s32[]{:T(128)} %get-tuple-element.124, bf16[2,512,16,64]{1,3,2,0:T(8,128)(2,1)} %get-tuple-element.135), kind=kOutput, calls=%fused_computation.82.clone.1 | convolution fusion | flops 549454336 | bytes 18908672 | tf_op jit(solution)/shard_map/while/body/eval_jaxpr/sub | solution.py:24
  228.1 9.2 %fusion.86 = bf16[2,512,16,64]{1,3,2,0:T(8,128)(2,1)} fusion(bf16[2,512,16,64]{1,3,2,0:T(8,128)(2,1)} %get-tuple-element.125, s32[]{:T(128)} %get-tuple-element.124, f32[16,512,512]{1,2,0:T(8,128)} %get-tuple-element.115, f32[16,512]{1,0:T(8,128)S(1)} %get-tuple-element.116, bf16[2,512,16,64]{1,3,2,0:T(8,128)(2,1)} %get-tuple-element.133), kind=kOutput, calls=%fused_computation.14.clone.1 | convolution fusion | flops 545783808 | bytes 18908160 | tf_op jit(solution)/shard_map/while/body/eval_jaxpr/hqk,khd->qhd/dot_general | solution.py:25
  237.3 3.8 copy.33
  241.1 1.9 copy.42
  243.1 0.0 copy-start.7
  243.1 9.2 %select_reduce_fusion.1 = f32[2,2048]{1,0:T(2,128)S(1)} fusion(pred[2,512]{1,0:T(4,128)(4,1)S(1)} %copy-done.4, bf16[1024,1024]{0,1:T(8,128)(2,1)} %bitcast.103, bf16[1024,2048]{1,0:T(8,128)(2,1)} %all-gather.11.cloned.1.call-done, bf16[2,512,2048]{2,1,0:T(8,128)(2,1)} %param.12), kind=kOutput, calls=%fused_computation.40 | convolution fusion | flops 4303351808 | bytes 10503168 | tf_op jit(solution)/shard_map/dot_general | solution.py:54
  252.3 0.2 multiply_reduce_fusion
  252.6 0.7 fusion.55
  253.2 0.0 all-gather.13.cloned.1.call-update
  253.3 0.0 all-reduce.4.cloned.1.call-start
  253.3 0.0 copy-done.2
  253.3 0.1 copy.26
  253.5 0.2 dynamic-update-slice
  253.7 63.0 %all-reduce = s32[256]{0:T(256)S(1)} all-reduce(s32[256]{0:T(256)S(1)} %dynamic-update-slice), channel_id=1, replica_groups=mesh['dp'=128] {'dp'}, use_global_device_ids=true, to_apply=%add | all-reduce | flops 256 | bytes 2048
  316.7 0.7 gather_fusion
  317.4 0.1 fusion.51
  317.6 0.1 reshape.185
  317.7 3.2 sort.17
  320.9 0.1 compare_select_fusion.3
  320.9 2.3 reshape.196
  323.2 2.0 fusion.66
  325.2 129.5 %gather_fusion.2 = f32[16384]{0:T(1024)S(1)} fusion(f32[256,512]{1,0:T(8,128)S(1)} %fusion.66, s32[16384]{0:T(1024)S(1)} %reshape.185), kind=kCustom, calls=%fused_computation.2 | custom fusion | bytes 262144 | tf_op jit(solution)/shard_map/jit(take_along_axis)/gather | solution.py:78
  454.7 0.1 reshape.188
  454.7 0.8 select_select_fusion
  455.5 0.0 all-reduce.4.cloned.1.call-update
  455.6 139.4 %all-reduce.4.cloned.1.call-done = f32[256,64]{1,0:T(8,128)} async-done(((f32[256,64]{1,0:T(8,128)}), f32[256,64]{1,0:T(8,128)}) %all-reduce.4.cloned.1.call-update) | async-done | bytes 65552
  595.0 0.7 dynamic-slice_bitcast_fusion
  595.7 33.8 %all-gather.1 = f32[128,2,64]{2,1,0:T(2,128)S(1)} all-gather(f32[1,2,64]{2,1,0:T(2,128)S(1)} %dynamic-slice_bitcast_fusion), channel_id=1, replica_groups=mesh['dp'=128] {'dp'}, dimensions={0}, use_global_device_ids=true | all-gather | bytes 66048 | tf_op jit(solution)/shard_map/all_gather | solution.py:82
  629.5 1.1 gather_fusion.1
  (23 shorter events, 0.1 us)
Async XLA Ops:
  6.5 316.7 %copy-start = (bf16[512,2048]{1,0:T(8,128)(2,1)S(1)}, bf16[512,2048]{1,0:T(8,128)(2,1)}, u32[]{:S(2)}) copy-start(bf16[512,2048]{1,0:T(8,128)(2,1)} %param.21) | copy-start | bytes 6291460
  6.5 100.3 %all-gather.7.cloned.1.call-start = ((), (), s32[]{:S(2)}) async-start(), calls=%async_computation.1 | async-start | bytes 4227072 | tf_op jit(solution)/shard_map/all_gather | solution.py:43
  7.3 166.8 %all-gather.9.cloned.1.call-start = ((), (), s32[]{:S(2)}) async-start(), calls=%async_computation.2 | async-start | bytes 4227072 | tf_op jit(solution)/shard_map/all_gather | solution.py:42
  11.3 65.0 %all-to-all-start = ((bf16[128,16,1024]{2,1,0:T(8,128)(2,1)}), bf16[128,16,1024]{2,1,0:T(8,128)(2,1)}, u32[]{:S(2)}, u32[]{:S(2)}) async-start(bf16[128,16,1024]{2,1,0:T(8,128)(2,1)} %stack.2), calls=%async_computation | async-start | bytes 8388608 | tf_op jit(solution)/shard_map/all_to_all | solution.py:14
  23.2 3.9 copy-start.6
  23.2 5.2 copy-start.3
  23.2 219.8 %all-gather.11.cloned.1.call-start = ((), (), s32[]{:S(2)}) async-start(), calls=%async_computation.3 | async-start | bytes 4227072 | tf_op jit(solution)/shard_map/all_gather | solution.py:55
  24.0 297.0 %all-gather.13.cloned.1.call-start = ((), (), s32[]{:S(2)}) async-start(), calls=%async_computation.4 | async-start | bytes 1056768 | tf_op jit(solution)/shard_map/all_gather | solution.py:71
  28.4 5.3 copy-start.1
  237.3 5.7 copy-start.4
  243.1 9.3 %copy-start.5 = (f32[2]{0:T(128)S(1)}, f32[2]{0:T(128)}, u32[]{:S(2)}) copy-start(f32[2]{0:T(128)} %convert_element_type.51) | copy-start | bytes 28
  243.1 10.3 %copy-start.2 = (s32[256,64]{0,1:T(8,128)S(1)}, s32[256,64]{0,1:T(8,128)}, u32[]{:S(2)}) copy-start(s32[256,64]{0,1:T(8,128)} %param.15) | copy-start | bytes 196612
  243.1 10.4 %copy-start.7 = (s32[2]{0:T(128)S(1)}, s32[2]{0:T(128)}, u32[]{:S(2)}) copy-start(s32[2]{0:T(128)} %param.14) | copy-start | bytes 28
  253.3 341.7 %all-reduce.4.cloned.1.call-start = ((), (), s32[]{:S(2)}) async-start(), calls=%async_computation.5 | async-start | bytes 262144
Sparse Core Ops, SparseCore 0:
  10.5 96.3 all-gather.6
  110.0 64.0 all-gather.8
  177.2 64.1 all-gather.10
  253.4 61.1 all-gather.12
  455.7 139.2 all-reduce.3
